TPU v7x, 32 devices: a whole 2x2x4 slice. The times are simulated.
32 devices in a mesh: expert: 4 (over z), dp: 4 (over y, core), replica: 2 (over x).
Axes of the slice: x: 2, y: 2, z: 4, core: 2. Of those that a mesh axis runs over, the one named last changes fastest.
Arguments:
- cotangent: bfloat16 [2, 4, 4, 128, 2048], P('replica', 'expert', 'dp'), may hold values from -0.5 to 0.5
- expert_ids: int32 [2, 4, 4, 128, 2], P('replica', 'expert', 'dp'), may hold values from 0 to 3, all different within a row; in each aligned block of 128 rows (0 to 127, 128 to 255, ..., all dimensions but the last counted through in order) at most 96 rows name the same one
- gate_values: float32 [2, 4, 4, 128, 2], P('replica', 'expert', 'dp'), may hold values from 0.1 to 1
- hidden_saved: bfloat16 [2, 4, 4, 4, 4, 24, 7168], P('replica', 'expert', 'dp'), may hold values from -6 to 6
- output_saved: bfloat16 [2, 4, 4, 4, 4, 24, 2048], P('replica', 'expert', 'dp'), may hold values from -6 to 6
- weights: bfloat16 [2, 4, 7168, 2048], P('replica', 'expert', 'dp'), may hold values from -6 to 6
- moment_one: bfloat16 [2, 4, 7168, 2048], P('replica', 'expert', 'dp'), may hold values from -4 to 4
- moment_two: bfloat16 [2, 4, 7168, 2048], P('replica', 'expert', 'dp'), may hold values from 0.19921875 to 2
- anchor: float32 [4, 1792, 2048], P('expert', 'dp'), may hold values from -6 to 6
- outer_moment: float32 [4, 1792, 2048], P('expert', 'dp'), may hold values from -2 to 2
Outputs:
- new_weights: bfloat16 [2, 4, 7168, 2048], P('replica', 'expert', 'dp')
- gate_grads: float32 [2, 4, 4, 128, 2], P('replica', 'expert', 'dp')
- grad_rms: float32 [2], P('replica')
Inputs may be any that keep to these rules, and one draw needn't show every extreme that they name: `expert_ids`: each token names two different experts; among the 128 tokens of one device no expert is named more than 96 times, a bound that some block reaches.
All inputs are finite; a program needn't handle non-finite values.
Results may differ from a plain program's by a relative error of at most 0.0075.
Values may be sent and summed in bfloat16 or wider, within the bound.
A program may use at most 192 MiB of HBM per device.

v0:
```python
import jax
import jax.numpy as jnp
from jax import lax
from jax.sharding import PartitionSpec as P

beta_one = 0.9
beta_two = 0.95
epsilon = 1e-08
inner_rate = 0.3
weight_decay = 0.1
outer_rate = 0.7
nesterov_coef = 0.9


def shards(
    cotangent,
    expert_ids,
    gate_values,
    hidden_saved,
    output_saved,
    weights,
    moment_one,
    moment_two,
    anchor,
    outer_moment,
):
    n_exp = lax.axis_size("expert")
    n_dp = lax.axis_size("dp")
    n_rep = lax.axis_size("replica")
    tok_rows = cotangent.shape[3]
    model_width = cotangent.shape[4]
    capacity = hidden_saved.shape[5]
    hidden_width = hidden_saved.shape[6]
    slots_dev = n_exp * n_dp * capacity
    shard_rows = hidden_width // n_dp
    chosen = expert_ids.reshape(-1)
    onehot = (chosen[:, None] == jnp.arange(n_exp, dtype=jnp.int32)[None, :]).astype(jnp.int32)
    before = jnp.cumsum(onehot, axis=0) - onehot
    order_rank = jnp.sum(before * onehot, axis=1)
    position = (chosen * n_dp + order_rank % n_dp) * capacity + order_rank // n_dp
    stored = output_saved.reshape(n_exp, n_dp, capacity, model_width)
    returned = lax.all_to_all(
        stored.reshape(n_exp * n_dp, capacity, model_width),
        ("expert", "dp"),
        split_axis=0,
        concat_axis=0,
        tiled=True,
    )
    picked = jnp.take(returned.reshape(slots_dev, model_width), position, axis=0).reshape(
        tok_rows, 2, model_width
    )
    upstream = cotangent.reshape(tok_rows, model_width)
    gate_grads = jnp.einsum("tkd,td->tk", picked, upstream, preferred_element_type=jnp.float32)
    gates = gate_values.reshape(tok_rows, 2)
    sends = (gates[:, :, None] * upstream[:, None, :].astype(jnp.float32)).astype(jnp.bfloat16)
    buffer = (
        jnp.zeros((slots_dev, model_width), jnp.bfloat16)
        .at[position]
        .set(sends.reshape(2 * tok_rows, model_width))
    )
    arrived = lax.all_to_all(
        buffer.reshape(n_exp * n_dp, capacity, model_width),
        ("expert", "dp"),
        split_axis=0,
        concat_axis=0,
        tiled=True,
    )
    arrived = arrived.reshape(slots_dev, model_width)
    hidden = hidden_saved.reshape(slots_dev, hidden_width)
    gradient = lax.psum_scatter(
        lax.dot_general(
            hidden, arrived, (((0,), (0,)), ((), ())), preferred_element_type=jnp.float32
        ).astype(jnp.bfloat16),
        "dp",
        scatter_dimension=0,
        tiled=True,
    ).astype(jnp.float32)
    squares = lax.psum(jnp.sum(gradient * gradient), ("expert", "dp"))
    grad_rms = jnp.sqrt(squares / (n_exp * hidden_width * model_width)).reshape(1)
    weight_old = weights.reshape(shard_rows, model_width).astype(jnp.float32)
    first_new = (
        beta_one * moment_one.reshape(shard_rows, model_width).astype(jnp.float32)
        + (1.0 - beta_one) * gradient
    )
    second_new = (
        beta_two * moment_two.reshape(shard_rows, model_width).astype(jnp.float32)
        + (1.0 - beta_two) * gradient * gradient
    )
    inner_new = weight_old - inner_rate * (
        first_new / (jnp.sqrt(second_new) + epsilon) + weight_decay * weight_old
    )
    inner_new = inner_new.astype(jnp.bfloat16)
    grouped = inner_new.reshape(shard_rows // 4, 4, model_width)
    fragment = grouped[:, 0, :].astype(jnp.float32)
    start_point = anchor.reshape(shard_rows // 4, model_width)
    summed = lax.psum((start_point - fragment).astype(jnp.bfloat16), "replica").astype(jnp.float32)
    average = summed / n_rep
    momentum = nesterov_coef * outer_moment.reshape(shard_rows // 4, model_width) + average
    new_anchor = start_point - outer_rate * (average + nesterov_coef * momentum)
    updated = (
        grouped.at[:, 0, :]
        .set(new_anchor.astype(jnp.bfloat16))
        .reshape(1, 1, shard_rows, model_width)
    )
    return (updated, gate_grads.reshape(1, 1, 1, tok_rows, 2), grad_rms)


def solution(mesh):
    return jax.shard_map(
        shards,
        mesh=mesh,
        in_specs=(
            P("replica", "expert", "dp", None, None),
            P("replica", "expert", "dp", None, None),
            P("replica", "expert", "dp", None, None),
            P("replica", "expert", "dp", None, None, None, None),
            P("replica", "expert", "dp", None, None, None, None),
            P("replica", "expert", "dp", None),
            P("replica", "expert", "dp", None),
            P("replica", "expert", "dp", None),
            P("expert", "dp", None),
            P("expert", "dp", None),
        ),
        out_specs=(
            P("replica", "expert", "dp", None),
            P("replica", "expert", "dp", None, None),
            P("replica"),
        ),
        check_vma=False,
    )
```

profile of v0, /device:TPU:0, one launch (start us, length us, event | category | flops | bytes accessed | tf_op | source)
XLA Modules:
  0.0 495.1 jit_solution(3797463655363721530)
XLA Ops:
  7.2 0.8 copy.35
  8.1 0.1 eq.27
  8.3 1.2 reduce-window.6
  9.9 0.1 mul.129
  10.1 1.1 bitcast_convert_fusion
  11.2 2.5 mul.136
  13.7 2.7 mul.137
  16.6 0.1 mul.134
  16.7 3.5 scatter_custom_fusion
  20.2 43.5 %all_to_all.10 = bf16[16,24,2048]{2,1,0:T(8,128)(2,1)S(1)} all-to-all(bf16[16,24,2048]{2,1,0:T(8,128)(2,1)} %bitcast.83), channel_id=1, replica_groups=mesh['expert'=4,'dp'=4,'replica'=2] {'expert','dp'}, dimensions={0} | all-to-all | bytes 3145728 | tf_op jit(solution)/shard_map/all_to_all | solution.py:61
  63.7 21.7 %convert_bitcast_fusion = bf16[7168,2048]{0,1:T(8,128)(2,1)} fusion(bf16[384,2048]{1,0:T(8,128)(2,1)S(1)} %bitcast.85, bf16[384,7168]{1,0:T(8,128)(2,1)} %bitcast.92), kind=kOutput, calls=%fused_computation.2 | convolution fusion | flops 11288969216 | bytes 36438016 | tf_op jit(solution)/shard_map/dot_general | solution.py:71
  85.4 5.0 %all-to-all-start.1 = ((bf16[16,24,2048]{2,1,0:T(8,128)(2,1)}), bf16[16,24,2048]{2,1,0:T(8,128)(2,1)S(1)}, u32[]{:S(2)}, u32[]{:S(2)}) async-start(bf16[16,24,2048]{2,1,0:T(8,128)(2,1)} %bitcast.84), calls=%async_computation.2 | async-start | bytes 3145728 | tf_op jit(solution)/shard_map/all_to_all | solution.py:42
  90.5 0.2 all-reduce.2.cloned.1.call-start
  90.7 10.7 %copy.33 = bf16[1,1,1792,2048]{2,3,1,0:T(8,128)(2,1)} copy(bf16[1,1,1792,2048]{3,2,1,0:T(8,128)(2,1)} %param.17) | data formatting | bytes 14680064 | tf_op args[5]
  101.4 11.0 %copy.34 = bf16[1,1,1792,2048]{2,3,1,0:T(8,128)(2,1)} copy(bf16[1,1,1792,2048]{3,2,1,0:T(8,128)(2,1)} %param.18) | data formatting | bytes 14680064 | tf_op args[6]
  112.4 10.8 %copy.41 = bf16[1,1,1792,2048]{2,3,1,0:T(8,128)(2,1)} copy(bf16[1,1,1792,2048]{3,2,1,0:T(8,128)(2,1)} %param.19) | data formatting | bytes 14680064 | tf_op args[7]
  123.2 170.8 %reduce-scatter.2.cloned.1.call-done = bf16[1792,2048]{0,1:T(8,128)(2,1)} async-done(((bf16[7168,2048]{0,1:T(8,128)(2,1)}), bf16[1792,2048]{0,1:T(8,128)(2,1)}) %reduce-scatter.2.cloned.1.call-update) | async-done | bytes 7340048 | tf_op jit(solution)/shard_map/reduce_scatter | solution.py:70
  294.0 18.8 %fusion.8 = (f32[]{:T(128)}, bf16[1792,2048]{0,1:T(8,128)(2,1)}) fusion(bf16[1792,2048]{0,1:T(8,128)(2,1)} %reduce-scatter.2.cloned.1.call-done, bf16[1,1,1792,2048]{2,3,1,0:T(8,128)(2,1)} %copy.41, bf16[1,1,1792,2048]{2,3,1,0:T(8,128)(2,1)} %copy.34, bf16[1,1,1792,2048]{2,3,1,0:T(8,128)(2,1)} %copy.33), kind=kLoop, calls=%fused_computation.17 | loop fusion | flops 73400320 | bytes 36700164 | tf_op jit(solution)/shard_map/reduce_sum | solution.py:78
  312.7 10.2 %copy.42 = bf16[1792,2048]{1,0:T(8,128)(2,1)} copy(bf16[1792,2048]{0,1:T(8,128)(2,1)} %get-tuple-element.16) | data formatting | bytes 14680064 | tf_op jit(solution)/shard_map/convert_element_type | solution.py:92
  322.9 11.6 %reshape.232 = bf16[448,4,2048]{2,1,0:T(4,128)(2,1)} reshape(bf16[1792,2048]{1,0:T(8,128)(2,1)} %copy.42) | data formatting | bytes 14680064 | tf_op jit(solution)/shard_map/reshape | solution.py:93
  334.5 8.0 %slice_convert_fusion = f32[448,1,2048]{2,1,0:T(1,128)} fusion(bf16[448,4,2048]{2,1,0:T(4,128)(2,1)} %reshape.232), kind=kLoop, calls=%fused_computation.18 | loop fusion | flops 917504 | bytes 5505024 | tf_op jit(solution)/shard_map/convert_element_type | solution.py:94
  342.5 5.6 %fusion.9 = bf16[448,2048]{1,0:T(8,128)(2,1)} fusion(f32[448,1,2048]{2,1,0:T(1,128)} %slice_convert_fusion, f32[1,448,2048]{2,1,0:T(8,128)} %param.20), kind=kLoop, calls=%fused_computation.20 | loop fusion | flops 1835008 | bytes 9175040 | tf_op jit(solution)/shard_map/convert_element_type | solution.py:96
  348.4 1.4 gather_fusion
  349.8 0.7 gather.7
  350.5 3.8 fusion.18
  354.3 0.7 copy.45
  355.0 32.8 %psum.15 = f32[]{:T(128)} all-reduce(f32[]{:T(128)} %get-tuple-element.15), channel_id=1, replica_groups=mesh['expert'=4,'dp'=4,'replica'=2] {'expert','dp'}, use_global_device_ids=true, to_apply=%region_7.8 | all-reduce | flops 1 | bytes 8 | tf_op jit(solution)/shard_map/psum | solution.py:78
  388.5 17.1 %all-reduce.2.cloned.1.call-done = bf16[448,2048]{1,0:T(8,128)(2,1)} async-done(((bf16[448,2048]{1,0:T(8,128)(2,1)}), bf16[448,2048]{1,0:T(8,128)(2,1)}) %all-reduce.2.cloned.1.call-update) | async-done | bytes 1835024 | tf_op jit(solution)/shard_map/psum | solution.py:96
  405.6 4.8 fusion.15
  410.4 4.7 copy.43
  415.1 61.0 %scatter.13 = bf16[448,4,2048]{2,1,0:T(4,128)(2,1)} dynamic-update-slice(bf16[448,4,2048]{2,1,0:T(4,128)(2,1)} %reshape.232, bf16[448,1,2048]{2,1,0:T(2,128)(2,1)} %copy.43, s32[]{:T(128)} %constant.88.clone.1, s32[]{:T(128)} %constant.88.clone.1, s32[]{:T(128)} %constant.88.clone.1) | dynamic-update-slice | bytes 3670020 | tf_op jit(solution)/shard_map/scatter | solution.py:102
  476.1 11.0 %reshape.235 = bf16[1,1,1792,2048]{3,2,1,0:T(8,128)(2,1)} reshape(bf16[448,4,2048]{2,1,0:T(4,128)(2,1)} %scatter.13) | data formatting | bytes 14680064 | tf_op jit(solution)/shard_map/reshape | solution.py:103
  (23 shorter events, 1.0 us)
Async XLA Ops:
  7.2 9.3 %copy-start.1 = (f32[1,1,1,128,2]{3,4,2,1,0:T(2,128)S(1)}, f32[1,1,1,128,2]{3,4,2,1,0:T(2,128)}, u32[]{:S(2)}) copy-start(f32[1,1,1,128,2]{3,4,2,1,0:T(2,128)} %param.14) | copy-start | bytes 3076
  7.2 286.8 %reduce-scatter.2.cloned.1.call-start = ((), (), s32[]{:S(2)}) async-start(), calls=%async_computation.3 | async-start | bytes 36700160 | tf_op jit(solution)/shard_map/reduce_scatter | solution.py:70
  85.4 263.0 %all-to-all-start.1 = ((bf16[16,24,2048]{2,1,0:T(8,128)(2,1)}), bf16[16,24,2048]{2,1,0:T(8,128)(2,1)S(1)}, u32[]{:S(2)}, u32[]{:S(2)}) async-start(bf16[16,24,2048]{2,1,0:T(8,128)(2,1)} %bitcast.84), calls=%async_computation.2 | async-start | bytes 3145728 | tf_op jit(solution)/shard_map/all_to_all | solution.py:42
  90.5 315.1 %all-reduce.2.cloned.1.call-start = ((), (), s32[]{:S(2)}) async-start(), calls=%async_computation.4 | async-start | bytes 3670016 | tf_op jit(solution)/shard_map/psum | solution.py:96
  348.4 2.1 copy-start
Sparse Core Ops, SparseCore 0:
  85.5 208.3 reduce-scatter.1
  348.3 57.2 all-reduce.1
where the time goes:
time: 501 us; the launch traced here: 495 us
  waiting for transfers between devices  188 us (38%)
  local copies, waits for them, and re-layouts  141 us (28%)
  blocking collectives  76.3 us (15%)
  other arithmetic  43.3 us (9%)
  matrix products  25.4 us (5%)
  between operations  16 us (3%)
  starting transfers between devices  5.3 us (1%)
    reduce_scatter x1, waiting for transfers between devices, shards(): lax.psum_scatter(lax.dot_general(hidden, arrived, (((0,), (0,)), ((), ())...  171 us
    scatter x1, local copies, waits for them, and re-layouts, shards(): updated = grouped.at[:, 0, :].set(new_anchor.astype(jnp.bfloat16)).reshap...  61 us
    all_to_all x1, blocking collectives, shards(): lax.all_to_all(buffer.reshape(n_exp * n_dp, capacity, model_width), ('exp...  43.5 us
    unnamed x9, local copies, waits for them, and re-layouts  33.4 us
    psum x1, blocking collectives, shards(): squares = lax.psum(jnp.sum(gradient * gradient), ('expert', 'dp'))  32.8 us
    dot_general x1, matrix products, shards(): lax.dot_general(hidden, arrived, (((0,), (0,)), ((), ())), preferred_elem...  21.7 us
    reduce_sum x1, other arithmetic, shards(): squares = lax.psum(jnp.sum(gradient * gradient), ('expert', 'dp'))  18.8 us
    psum x1, waiting for transfers between devices, shards(): lax.psum((start_point - fragment).astype(jnp.bfloat16), 'replica')  17.1 us
  transfers between devices with their start and end apart: 3, of which 2 were waited for; matrix products, arithmetic and copies ran while one was open for 19% of the time, Pallas kernels for 0%

commit v1 on v0

--- a/solution.py
+++ b/solution.py
@@ -10,6 +10,18 @@
 weight_decay = 0.1
 outer_rate = 0.7
 nesterov_coef = 0.9
+
+
+def split_up(x, dim, size):
+    lengths = x.shape
+    blocks = x.reshape(*lengths[:dim], size, lengths[dim] // size, *lengths[dim + 1 :])
+    return jnp.moveaxis(blocks, dim, 0)
+
+
+def laid_out(blocks, dim):
+    blocks = jnp.moveaxis(blocks, 0, dim)
+    shape = blocks.shape
+    return blocks.reshape(*shape[:dim], shape[dim] * shape[dim + 1], *shape[dim + 2 :])
 
 
 def shards(
@@ -58,13 +70,17 @@
         .at[position]
         .set(sends.reshape(2 * tok_rows, model_width))
     )
-    arrived = lax.all_to_all(
-        buffer.reshape(n_exp * n_dp, capacity, model_width),
-        ("expert", "dp"),
-        split_axis=0,
-        concat_axis=0,
-        tiled=True,
-    )
+    x = buffer.reshape(n_exp * n_dp, capacity, model_width)
+    size, mine = (lax.axis_size(("expert", "dp")), lax.axis_index(("expert", "dp")))
+    blocks = split_up(x, 0, size)
+    finished = [blocks[mine]]
+    for lap in range(1, size):
+        sent = blocks[(mine + lap) % size]
+        finished.append(
+            lax.ppermute(sent, ("expert", "dp"), [(i, (i + lap) % size) for i in range(size)])
+        )
+    blocks = jnp.stack(finished)[(mine - jnp.arange(size)) % size]
+    arrived = laid_out(blocks, 0)
     arrived = arrived.reshape(slots_dev, model_width)
     hidden = hidden_saved.reshape(slots_dev, hidden_width)
     gradient = lax.psum_scatter(

time: 501 us -> 507 us (1.012)
  blocking collectives: 76.3 us -> 32.9 us
  starting transfers between devices: 5.3 us -> 33.7 us
  waiting for transfers between devices: 188 us -> 203 us
    all_to_all x1 -> x0, blocking collectives: 43.5 us -> none  [shards(): lax.all_to_all(buffer.reshape(n_exp * n_dp, capacity, model_width), ('exp...]
    ppermute x0 -> x15, starting transfers between devices: none -> 27.4 us  [shards(): lax.ppermute(sent, ('expert', 'dp'), [(i, (i + lap) % size) for i in rang...]
    ppermute x0 -> x15, waiting for transfers between devices: none -> 15.4 us  [shards(): lax.ppermute(sent, ('expert', 'dp'), [(i, (i + lap) % size) for i in rang...]
    unnamed x9 -> x23, local copies, waits for them, and re-layouts: 33.4 us -> 33.7 us
  transfers between devices with their start and end apart: 3 -> 18, of which waited for: 2 -> 8; matrix products, arithmetic and copies ran while one was open for 19% -> 19% of each run, Pallas kernels for 0% -> 0%
where the time goes in v1:
time: 507 us; the launch traced here: 500 us
  waiting for transfers between devices  203 us (40%)
  local copies, waits for them, and re-layouts  145 us (29%)
  other arithmetic  43.3 us (9%)
  starting transfers between devices  33.7 us (7%)
  blocking collectives  32.9 us (6%)
  matrix products  25.9 us (5%)
  between operations  16.4 us (3%)
    reduce_scatter x1, waiting for transfers between devices, shards(): lax.psum_scatter(lax.dot_general(hidden, arrived, (((0,), (0,)), ((), ())...  171 us
    scatter x1, local copies, waits for them, and re-layouts, shards(): updated = grouped.at[:, 0, :].set(new_anchor.astype(jnp.bfloat16)).reshap...  61.3 us
    unnamed x23, local copies, waits for them, and re-layouts  33.7 us
    psum x1, blocking collectives, shards(): squares = lax.psum(jnp.sum(gradient * gradient), ('expert', 'dp'))  32.9 us
    ppermute x15, starting transfers between devices, shards(): lax.ppermute(sent, ('expert', 'dp'), [(i, (i + lap) % size) for i in rang...  27.4 us
    dot_general x1, matrix products, shards(): lax.dot_general(hidden, arrived, (((0,), (0,)), ((), ())), preferred_elem...  22.4 us
    reduce_sum x1, other arithmetic, shards(): squares = lax.psum(jnp.sum(gradient * gradient), ('expert', 'dp'))  18.8 us
    psum x1, waiting for transfers between devices, shards(): lax.psum((start_point - fragment).astype(jnp.bfloat16), 'replica')  17 us
  transfers between devices with their start and end apart: 18, of which 8 were waited for; matrix products, arithmetic and copies ran while one was open for 19% of the time, Pallas kernels for 0%

profile of v1, /device:TPU:0, one launch (start us, length us, event | category | flops | bytes accessed | tf_op | source)
XLA Modules:
  0.0 500.5 jit_solution(17669759072658775769)
XLA Ops:
  11.4 2.5 mul.139
  13.9 2.7 mul.140
  17.0 3.5 scatter_custom_fusion
  20.5 1.6 dynamic-slice_bitcast_fusion
  22.6 2.6 collective-permute-start.1
  25.2 2.4 collective-permute-start.2
  27.6 1.6 collective-permute-start.3
  31.4 3.6 collective-permute-start.6
  36.7 11.0 %collective-permute-done.4 = bf16[1,24,2048]{2,1,0:T(8,128)(2,1)S(1)} collective-permute-done((bf16[1,24,2048]{2,1,0:T(8,128)(2,1)S(1)}, bf16[1,24,2048]{2,1,0:T(8,128)(2,1)S(1)}, u32[]{:S(2)}, u32[]{:S(2)}) %collective-permute-start.4) | collective-permute-done | bytes 98336 | tf_op jit(solution)/shard_map/ppermute | solution.py:80
  47.9 3.0 collective-permute-start.10
  50.9 4.3 collective-permute-start.11
  56.8 3.7 collective-permute-start.13
  60.5 1.7 collective-permute-start.14
  65.2 1.8 gather_fusion
  67.0 22.4 %convert_bitcast_fusion = bf16[7168,2048]{0,1:T(8,128)(2,1)} fusion(bf16[384,2048]{1,0:T(8,128)(2,1)} %bitcast.149, bf16[384,7168]{1,0:T(8,128)(2,1)} %bitcast.156), kind=kOutput, calls=%fused_computation.3 | convolution fusion | flops 11288969216 | bytes 36438016 | tf_op jit(solution)/shard_map/dot_general | solution.py:87
  89.3 6.0 %all-to-all-start = ((bf16[16,24,2048]{2,1,0:T(8,128)(2,1)}), bf16[16,24,2048]{2,1,0:T(8,128)(2,1)S(1)}, u32[]{:S(2)}, u32[]{:S(2)}) async-start(bf16[16,24,2048]{2,1,0:T(8,128)(2,1)} %bitcast.148), calls=%async_computation.1 | async-start | bytes 3145728 | tf_op jit(solution)/shard_map/all_to_all | solution.py:54
  95.6 10.8 %copy.33 = bf16[1,1,1792,2048]{2,3,1,0:T(8,128)(2,1)} copy(bf16[1,1,1792,2048]{3,2,1,0:T(8,128)(2,1)} %param.17) | data formatting | bytes 14680064 | tf_op args[5]
  106.4 10.9 %copy.34 = bf16[1,1,1792,2048]{2,3,1,0:T(8,128)(2,1)} copy(bf16[1,1,1792,2048]{3,2,1,0:T(8,128)(2,1)} %param.18) | data formatting | bytes 14680064 | tf_op args[6]
  117.3 10.8 %copy.41 = bf16[1,1,1792,2048]{2,3,1,0:T(8,128)(2,1)} copy(bf16[1,1,1792,2048]{3,2,1,0:T(8,128)(2,1)} %param.19) | data formatting | bytes 14680064 | tf_op args[7]
  128.0 170.8 %reduce-scatter.2.cloned.1.call-done = bf16[1792,2048]{0,1:T(8,128)(2,1)} async-done(((bf16[7168,2048]{0,1:T(8,128)(2,1)}), bf16[1792,2048]{0,1:T(8,128)(2,1)}) %reduce-scatter.2.cloned.1.call-update) | async-done | bytes 7340048 | tf_op jit(solution)/shard_map/reduce_scatter | solution.py:86
  298.9 18.8 %fusion.8 = (f32[]{:T(128)}, bf16[1792,2048]{0,1:T(8,128)(2,1)}) fusion(bf16[1792,2048]{0,1:T(8,128)(2,1)} %reduce-scatter.2.cloned.1.call-done, bf16[1,1,1792,2048]{2,3,1,0:T(8,128)(2,1)} %copy.41, bf16[1,1,1792,2048]{2,3,1,0:T(8,128)(2,1)} %copy.34, bf16[1,1,1792,2048]{2,3,1,0:T(8,128)(2,1)} %copy.33), kind=kLoop, calls=%fused_computation.18 | loop fusion | flops 73400320 | bytes 36700164 | tf_op jit(solution)/shard_map/reduce_sum | solution.py:94
  317.6 10.4 %copy.42 = bf16[1792,2048]{1,0:T(8,128)(2,1)} copy(bf16[1792,2048]{0,1:T(8,128)(2,1)} %get-tuple-element.16) | data formatting | bytes 14680064 | tf_op jit(solution)/shard_map/convert_element_type | solution.py:108
  328.0 11.6 %reshape.273 = bf16[448,4,2048]{2,1,0:T(4,128)(2,1)} reshape(bf16[1792,2048]{1,0:T(8,128)(2,1)} %copy.42) | data formatting | bytes 14680064 | tf_op jit(solution)/shard_map/reshape | solution.py:109
  339.6 8.0 %slice_convert_fusion = f32[448,1,2048]{2,1,0:T(1,128)} fusion(bf16[448,4,2048]{2,1,0:T(4,128)(2,1)} %reshape.273), kind=kLoop, calls=%fused_computation.19 | loop fusion | flops 917504 | bytes 5505024 | tf_op jit(solution)/shard_map/convert_element_type | solution.py:110
  347.7 5.6 %fusion.9 = bf16[448,2048]{1,0:T(8,128)(2,1)} fusion(f32[448,1,2048]{2,1,0:T(1,128)} %slice_convert_fusion, f32[1,448,2048]{2,1,0:T(8,128)} %param.20), kind=kLoop, calls=%fused_computation.21 | loop fusion | flops 1835008 | bytes 9175040 | tf_op jit(solution)/shard_map/convert_element_type | solution.py:112
  356.0 3.5 fusion.18
  360.1 32.9 %psum.15 = f32[]{:T(128)} all-reduce(f32[]{:T(128)} %get-tuple-element.15), channel_id=1, replica_groups=mesh['expert'=4,'dp'=4,'replica'=2] {'expert','dp'}, use_global_device_ids=true, to_apply=%region_7.8 | all-reduce | flops 1 | bytes 8 | tf_op jit(solution)/shard_map/psum | solution.py:94
  393.7 17.0 %all-reduce.2.cloned.1.call-done = bf16[448,2048]{1,0:T(8,128)(2,1)} async-done(((bf16[448,2048]{1,0:T(8,128)(2,1)}), bf16[448,2048]{1,0:T(8,128)(2,1)}) %all-reduce.2.cloned.1.call-update) | async-done | bytes 1835024 | tf_op jit(solution)/shard_map/psum | solution.py:112
  410.7 4.8 fusion.15
  415.5 4.7 copy.43
  420.1 61.3 %scatter.13 = bf16[448,4,2048]{2,1,0:T(4,128)(2,1)} dynamic-update-slice(bf16[448,4,2048]{2,1,0:T(4,128)(2,1)} %reshape.273, bf16[448,1,2048]{2,1,0:T(2,128)(2,1)} %copy.43, s32[]{:T(128)} %constant.185.clone.1, s32[]{:T(128)} %constant.185.clone.1, s32[]{:T(128)} %constant.185.clone.1) | dynamic-update-slice | bytes 3670020 | tf_op jit(solution)/shard_map/scatter | solution.py:118
  481.5 11.0 %reshape.276 = bf16[1,1,1792,2048]{3,2,1,0:T(8,128)(2,1)} reshape(bf16[448,4,2048]{2,1,0:T(4,128)(2,1)} %scatter.13) | data formatting | bytes 14680064 | tf_op jit(solution)/shard_map/reshape | solution.py:119
  (71 shorter events, 16.9 us)
Async XLA Ops:
  7.2 291.7 %reduce-scatter.2.cloned.1.call-start = ((), (), s32[]{:S(2)}) async-start(), calls=%async_computation.2 | async-start | bytes 36700160 | tf_op jit(solution)/shard_map/reduce_scatter | solution.py:86
  13.9 2.7 copy-start.1
  22.1 7.9 %collective-permute-start = (bf16[1,24,2048]{2,1,0:T(8,128)(2,1)S(1)}, bf16[1,24,2048]{2,1,0:T(8,128)(2,1)S(1)}, u32[]{:S(2)}, u32[]{:S(2)}) collective-permute-start(bf16[1,24,2048]{2,1,0:T(8,128)(2,1)S(1)} %get-tuple-element.31), channel_id=1, source_target_pairs={{0,2},{2,4},{4,6},{6,8},{8,10},{10,12},{12,14},{14,16},{16,18},{18... | collective-permute-start | bytes 294920 | tf_op jit(solution)/shard_map/ppermute | solution.py:80
  22.6 8.8 %collective-permute-start.1 = (bf16[1,24,2048]{2,1,0:T(8,128)(2,1)S(1)}, bf16[1,24,2048]{2,1,0:T(8,128)(2,1)S(1)}, u32[]{:S(2)}, u32[]{:S(2)}) collective-permute-start(bf16[1,24,2048]{2,1,0:T(8,128)(2,1)S(1)} %get-tuple-element.30), channel_id=1, source_target_pairs={{0,4},{2,6},{4,8},{6,10},{8,12},{10,14},{12,16},{14,18},{16,20},{1... | collective-permute-start | bytes 294920 | tf_op jit(solution)/shard_map/ppermute | solution.py:80
  25.2 9.8 %collective-permute-start.2 = (bf16[1,24,2048]{2,1,0:T(8,128)(2,1)S(1)}, bf16[1,24,2048]{2,1,0:T(8,128)(2,1)S(1)}, u32[]{:S(2)}, u32[]{:S(2)}) collective-permute-start(bf16[1,24,2048]{2,1,0:T(8,128)(2,1)S(1)} %get-tuple-element.29), channel_id=1, source_target_pairs={{0,6},{2,8},{4,10},{6,12},{8,14},{10,16},{12,18},{14,20},{16,22},{... | collective-permute-start | bytes 294920 | tf_op jit(solution)/shard_map/ppermute | solution.py:80
  27.6 7.8 %collective-permute-start.3 = (bf16[1,24,2048]{2,1,0:T(8,128)(2,1)S(1)}, bf16[1,24,2048]{2,1,0:T(8,128)(2,1)S(1)}, u32[]{:S(2)}, u32[]{:S(2)}) collective-permute-start(bf16[1,24,2048]{2,1,0:T(8,128)(2,1)S(1)} %get-tuple-element.28), channel_id=1, source_target_pairs={{0,8},{2,10},{4,12},{6,14},{8,16},{10,18},{12,20},{14,22},{16,24},... | collective-permute-start | bytes 294920 | tf_op jit(solution)/shard_map/ppermute | solution.py:80
  29.2 18.5 %collective-permute-start.4 = (bf16[1,24,2048]{2,1,0:T(8,128)(2,1)S(1)}, bf16[1,24,2048]{2,1,0:T(8,128)(2,1)S(1)}, u32[]{:S(2)}, u32[]{:S(2)}) collective-permute-start(bf16[1,24,2048]{2,1,0:T(8,128)(2,1)S(1)} %get-tuple-element.27), channel_id=1, source_target_pairs={{0,10},{2,12},{4,14},{6,16},{8,18},{10,20},{12,22},{14,24},{16,26}... | collective-permute-start | bytes 294920 | tf_op jit(solution)/shard_map/ppermute | solution.py:80
  30.1 17.9 %collective-permute-start.5 = (bf16[1,24,2048]{2,1,0:T(8,128)(2,1)S(1)}, bf16[1,24,2048]{2,1,0:T(8,128)(2,1)S(1)}, u32[]{:S(2)}, u32[]{:S(2)}) collective-permute-start(bf16[1,24,2048]{2,1,0:T(8,128)(2,1)S(1)} %get-tuple-element.26), channel_id=1, source_target_pairs={{0,12},{2,14},{4,16},{6,18},{8,20},{10,22},{12,24},{14,26},{16,28}... | collective-permute-start | bytes 294920 | tf_op jit(solution)/shard_map/ppermute | solution.py:80
  31.4 19.5 %collective-permute-start.6 = (bf16[1,24,2048]{2,1,0:T(8,128)(2,1)S(1)}, bf16[1,24,2048]{2,1,0:T(8,128)(2,1)S(1)}, u32[]{:S(2)}, u32[]{:S(2)}) collective-permute-start(bf16[1,24,2048]{2,1,0:T(8,128)(2,1)S(1)} %get-tuple-element.25), channel_id=1, source_target_pairs={{0,14},{2,16},{4,18},{6,20},{8,22},{10,24},{12,26},{14,28},{16,30}... | collective-permute-start | bytes 294920 | tf_op jit(solution)/shard_map/ppermute | solution.py:80
  35.0 20.2 %collective-permute-start.7 = (bf16[1,24,2048]{2,1,0:T(8,128)(2,1)S(1)}, bf16[1,24,2048]{2,1,0:T(8,128)(2,1)S(1)}, u32[]{:S(2)}, u32[]{:S(2)}) collective-permute-start(bf16[1,24,2048]{2,1,0:T(8,128)(2,1)S(1)} %get-tuple-element.24), channel_id=1, source_target_pairs={{0,16},{2,18},{4,20},{6,22},{8,24},{10,26},{12,28},{14,30},{16,0},... | collective-permute-start | bytes 294920 | tf_op jit(solution)/shard_map/ppermute | solution.py:80
  35.5 21.3 %collective-permute-start.8 = (bf16[1,24,2048]{2,1,0:T(8,128)(2,1)S(1)}, bf16[1,24,2048]{2,1,0:T(8,128)(2,1)S(1)}, u32[]{:S(2)}, u32[]{:S(2)}) collective-permute-start(bf16[1,24,2048]{2,1,0:T(8,128)(2,1)S(1)} %get-tuple-element.23), channel_id=1, source_target_pairs={{0,18},{2,20},{4,22},{6,24},{8,26},{10,28},{12,30},{14,0},{16,2},{... | collective-permute-start | bytes 294920 | tf_op jit(solution)/shard_map/ppermute | solution.py:80
  47.7 12.8 %collective-permute-start.9 = (bf16[1,24,2048]{2,1,0:T(8,128)(2,1)S(1)}, bf16[1,24,2048]{2,1,0:T(8,128)(2,1)S(1)}, u32[]{:S(2)}, u32[]{:S(2)}) collective-permute-start(bf16[1,24,2048]{2,1,0:T(8,128)(2,1)S(1)} %get-tuple-element.22), channel_id=1, source_target_pairs={{0,20},{2,22},{4,24},{6,26},{8,28},{10,30},{12,0},{14,2},{16,4},{1... | collective-permute-start | bytes 294920 | tf_op jit(solution)/shard_map/ppermute | solution.py:80
  47.9 14.4 %collective-permute-start.10 = (bf16[1,24,2048]{2,1,0:T(8,128)(2,1)S(1)}, bf16[1,24,2048]{2,1,0:T(8,128)(2,1)S(1)}, u32[]{:S(2)}, u32[]{:S(2)}) collective-permute-start(bf16[1,24,2048]{2,1,0:T(8,128)(2,1)S(1)} %get-tuple-element.21), channel_id=1, source_target_pairs={{0,22},{2,24},{4,26},{6,28},{8,30},{10,0},{12,2},{14,4},{16,6},{18... | collective-permute-start | bytes 294920 | tf_op jit(solution)/shard_map/ppermute | solution.py:80
  50.9 11.4 %collective-permute-start.11 = (bf16[1,24,2048]{2,1,0:T(8,128)(2,1)S(1)}, bf16[1,24,2048]{2,1,0:T(8,128)(2,1)S(1)}, u32[]{:S(2)}, u32[]{:S(2)}) collective-permute-start(bf16[1,24,2048]{2,1,0:T(8,128)(2,1)S(1)} %get-tuple-element.20), channel_id=1, source_target_pairs={{0,24},{2,26},{4,28},{6,30},{8,0},{10,2},{12,4},{14,6},{16,8},{18,... | collective-permute-start | bytes 294920 | tf_op jit(solution)/shard_map/ppermute | solution.py:80
  55.3 7.1 %collective-permute-start.12 = (bf16[1,24,2048]{2,1,0:T(8,128)(2,1)S(1)}, bf16[1,24,2048]{2,1,0:T(8,128)(2,1)S(1)}, u32[]{:S(2)}, u32[]{:S(2)}) collective-permute-start(bf16[1,24,2048]{2,1,0:T(8,128)(2,1)S(1)} %get-tuple-element.19), channel_id=1, source_target_pairs={{0,26},{2,28},{4,30},{6,0},{8,2},{10,4},{12,6},{14,8},{16,10},{18,... | collective-permute-start | bytes 294920 | tf_op jit(solution)/shard_map/ppermute | solution.py:80
  56.8 6.8 %collective-permute-start.13 = (bf16[1,24,2048]{2,1,0:T(8,128)(2,1)S(1)}, bf16[1,24,2048]{2,1,0:T(8,128)(2,1)S(1)}, u32[]{:S(2)}, u32[]{:S(2)}) collective-permute-start(bf16[1,24,2048]{2,1,0:T(8,128)(2,1)S(1)} %get-tuple-element.18), channel_id=1, source_target_pairs={{0,28},{2,30},{4,0},{6,2},{8,4},{10,6},{12,8},{14,10},{16,12},{18,... | collective-permute-start | bytes 294920 | tf_op jit(solution)/shard_map/ppermute | solution.py:80
  60.5 4.6 collective-permute-start.14
  89.3 264.2 %all-to-all-start = ((bf16[16,24,2048]{2,1,0:T(8,128)(2,1)}), bf16[16,24,2048]{2,1,0:T(8,128)(2,1)S(1)}, u32[]{:S(2)}, u32[]{:S(2)}) async-start(bf16[16,24,2048]{2,1,0:T(8,128)(2,1)} %bitcast.148), calls=%async_computation.1 | async-start | bytes 3145728 | tf_op jit(solution)/shard_map/all_to_all | solution.py:54
  95.4 315.3 %all-reduce.2.cloned.1.call-start = ((), (), s32[]{:S(2)}) async-start(), calls=%async_computation.3 | async-start | bytes 3670016 | tf_op jit(solution)/shard_map/psum | solution.py:112
  354.9 1.0 copy-start
Sparse Core Ops, SparseCore 0:
  89.5 209.3 reduce-scatter.1
  353.4 57.2 all-reduce.1
